TPU v7x, 32 devices: a whole 2x2x4 slice. The times are simulated.
32 devices in a mesh: dp: 4 (over y, core), mp: 8 (over z, x).
Axes of the slice: x: 2, y: 2, z: 4, core: 2. Of those that a mesh axis runs over, the one named last changes fastest.
Arguments:
- student_rows: bfloat16 [3072, 256], P('dp'), may hold values from -12 to 12
- teacher_rows: bfloat16 [3072, 256], P('dp'), may hold values from -12 to 12
- student_protos: bfloat16 [256, 65536], P(None, 'mp'), may hold values from -12 to 12
- teacher_protos: bfloat16 [256, 65536], P(None, 'mp'), may hold values from -12 to 12
- center: float32 [65536], P('mp'), may hold values from -0.25 to 0.25
- row_weight: float32 [3072], P('dp'), may hold values from 0.25 to 4
Outputs:
- grad_rows: float32 [3072, 256], P('dp')
- proto_grad: float32 [256, 65536], P('dp', 'mp')
All inputs are finite; a program needn't handle non-finite values.
Results may differ from a plain program's by a relative error of at most 0.012.
The roundings to bfloat16 on the way count: a program that leaves them out, or rounds other values in their place, can miss the bound.
Values sent between devices are 32-bit elements; how exact they have to be, the bound alone decides.
A program may use at most 192 MiB of HBM per device.

v0:
```python
import jax
import jax.numpy as jnp
from jax import lax
from jax.sharding import PartitionSpec as P

student_temp = 0.1
teacher_temp = 0.04
norm_eps = 1e-06


def local(student_rows, teacher_rows, student_protos, teacher_protos, center, row_weight):
    s_full = student_rows.astype(jnp.float32)
    row_norm = jnp.sqrt(jnp.sum(s_full * s_full, axis=1, keepdims=True) + norm_eps)
    z_unit = s_full / row_norm
    z_student = z_unit.astype(jnp.bfloat16)
    t_full = teacher_rows.astype(jnp.float32)
    z_teacher = (
        t_full / jnp.sqrt(jnp.sum(t_full * t_full, axis=1, keepdims=True) + norm_eps)
    ).astype(jnp.bfloat16)
    v_full = student_protos.astype(jnp.float32)
    col_norm = jnp.sqrt(jnp.sum(v_full * v_full, axis=0, keepdims=True) + norm_eps)
    w_student = (v_full / col_norm).astype(jnp.bfloat16)
    u_full = teacher_protos.astype(jnp.float32)
    w_teacher = (
        u_full / jnp.sqrt(jnp.sum(u_full * u_full, axis=0, keepdims=True) + norm_eps)
    ).astype(jnp.bfloat16)
    s_logit = jnp.dot(z_student, w_student, preferred_element_type=jnp.float32)
    t_logit = jnp.dot(z_teacher, w_teacher, preferred_element_type=jnp.float32)
    e_student = jnp.exp((s_logit - 1.0) / student_temp)
    e_teacher = jnp.exp((t_logit - center[None, :] - 1.0) / teacher_temp)
    sum_student, sum_teacher = lax.psum(
        (jnp.sum(e_student, axis=1), jnp.sum(e_teacher, axis=1)), "mp"
    )
    grad_logit = (
        row_weight[:, None]
        * (e_student / sum_student[:, None] - e_teacher / sum_teacher[:, None])
        / student_temp
    ).astype(jnp.bfloat16)
    partial_value = lax.dot_general(
        grad_logit, w_student, (((1,), (1,)), ((), ())), preferred_element_type=jnp.float32
    )
    grad_unit = lax.psum(partial_value, "mp")
    grad_rows = (grad_unit - z_unit * jnp.sum(z_unit * grad_unit, axis=1, keepdims=True)) / row_norm
    features = student_rows.shape[1]
    feature_rows = features // lax.axis_size("dp")
    grad_w = lax.psum_scatter(
        lax.dot_general(
            z_student, grad_logit, (((0,), (0,)), ((), ())), preferred_element_type=jnp.float32
        ),
        "dp",
        scatter_dimension=0,
        tiled=True,
    )
    w_mine = lax.dynamic_slice_in_dim(
        w_student, lax.axis_index("dp") * feature_rows, feature_rows, 0
    ).astype(jnp.float32)
    col_dot = lax.psum(jnp.sum(s_logit * grad_logit.astype(jnp.float32), axis=0), "dp")
    proto_grad = (grad_w - w_mine * col_dot[None, :]) / col_norm
    return (grad_rows, proto_grad)


def solution(mesh):
    placed = (P("dp", None), P("dp", None), P(None, "mp"), P(None, "mp"), P("mp"), P("dp"))
    return jax.shard_map(
        local, mesh=mesh, in_specs=placed, out_specs=(P("dp", None), P("dp", "mp")), check_vma=False
    )
```

profile of v0, /device:TPU:0, one launch (start us, length us, event | category | flops | bytes accessed | tf_op | source)
XLA Modules:
  0.0 183.0 jit_solution(13488176183522811870)
XLA Ops:
  8.0 0.0 copy-start.3
  8.0 0.0 copy-start.5
  8.0 0.0 all-reduce.3.cloned.1.call-start
  8.1 0.0 copy-start.4
  8.1 3.2 %fusion.2 = f32[8192]{0:T(1024)S(1)} fusion(bf16[256,8192]{1,0:T(8,128)(2,1)} %param.8), kind=kLoop, calls=%fused_computation.10 | loop fusion | flops 6283264 | bytes 4227072 | tf_op jit(solution)/shard_map/reduce_sum | solution.py:21
  11.3 3.2 %fusion.3 = bf16[256,8192]{1,0:T(8,128)(2,1)S(1)} fusion(bf16[256,8192]{1,0:T(8,128)(2,1)} %param.8, f32[8192]{0:T(1024)S(1)} %add_sqrt_fusion.1), kind=kLoop, calls=%fused_computation.11 | loop fusion | flops 6291456 | bytes 8421376 | tf_op jit(solution)/shard_map/convert_element_type | solution.py:22
  14.5 0.0 copy-done.3
  14.5 0.0 copy-start.1
  14.5 0.2 fusion.9
  14.7 0.0 copy-done.4
  14.7 0.9 fusion.4
  15.6 0.0 copy-done.5
  15.6 0.2 fusion.10
  15.8 0.7 copy-done.1
  16.5 0.0 copy-start.6
  16.5 11.1 %fusion = (f32[768]{0:T(1024)S(1)}, f32[768,8192]{1,0:T(8,128)}) fusion(bf16[256,8192]{1,0:T(8,128)(2,1)S(1)} %fusion.3, f32[768]{0:T(1024)S(1)} %add_sqrt_fusion.3, bf16[768,256]{1,0:T(8,128)(2,1)S(1)} %copy-done.3), kind=kOutput, calls=%fused_computation.4 | convolution fusion | flops 3240688896 | bytes 29759488 | tf_op jit(solution)/shard_map/dot_general | solution.py:27
  27.7 0.0 copy-done.6
  27.7 0.0 copy-start.7
  27.7 11.4 %fusion.1 = (f32[768]{0:T(1024)S(1)}, f32[768,8192]{1,0:T(8,128)}) fusion(f32[8192]{0:T(1024)S(1)} %copy-done.6, bf16[256,8192]{1,0:T(8,128)(2,1)S(1)} %copy-done.4, f32[8192]{0:T(1024)S(1)} %add_sqrt_fusion, bf16[768,256]{1,0:T(8,128)(2,1)S(1)} %copy-done.5, f32[768]{0:T(1024)S(1)} %add_sqrt_fusion.2), kind=kOutput, calls=%fused_computation.5 | convolution fusion | flops 3253271808 | bytes 29825024 | tf_op jit(solution)/shard_map/dot_general | solution.py:28
  39.0 23.5 %all-reduce = (f32[768]{0:T(1024)S(1)}, f32[768]{0:T(1024)S(1)}) all-reduce(f32[768]{0:T(1024)S(1)} %get-tuple-element.6, f32[768]{0:T(1024)S(1)} %get-tuple-element.8), channel_id=1, replica_groups=mesh['dp'=4,'mp'=8] {'mp'}, use_global_device_ids=true, to_apply=%region_7.0 | all-reduce | flops 1536 | bytes 12288 | tf_op jit(solution)/shard_map/psum | solution.py:31
  62.6 0.0 copy-done.7
  62.6 0.0 copy-start.2
  62.6 21.1 %multiply_reduce_fusion = (f32[8192]{0:T(1024)S(1)}, bf16[768,8192]{1,0:T(8,128)(2,1)S(1)}) fusion(f32[768,8192]{1,0:T(8,128)} %get-tuple-element.9, f32[768]{0:T(1024)S(1)} %get-tuple-element.2, f32[768,8192]{1,0:T(8,128)} %get-tuple-element.7, f32[8192]{0:T(1024)S(1)} %copy-done.6, f32[768]{0:T(1024)S(1)} %get-tuple-element.3, f32[768]{0:T(1024)S(1)} %copy-done.7), kind=kLoop, calls=%fused_computation | loop fusion | flops 88072192 | bytes 62989312 | tf_op jit(solution)/shard_map/reduce_sum | solution.py:57
  83.7 0.0 copy-start
  83.7 4.6 %copy-done = bf16[768,8192]{1,0:T(8,128)(2,1)} copy-done((bf16[768,8192]{1,0:T(8,128)(2,1)}, bf16[768,8192]{1,0:T(8,128)(2,1)S(1)}, u32[]{:S(2)}) %copy-start) | copy-done | bytes 12582936
  88.3 0.0 copy-done.2
  88.3 4.3 %fusion.18 = f32[768,256]{1,0:T(8,128)} fusion(bf16[768,8192]{1,0:T(8,128)(2,1)S(1)} %get-tuple-element.5, bf16[256,8192]{1,0:T(8,128)(2,1)S(1)} %copy-done.2), kind=kOutput, calls=%fused_computation.35 | convolution fusion | flops 3221225472 | bytes 17563648 | tf_op jit(solution)/shard_map/dot_general | solution.py:39
  92.6 0.0 all-reduce.3.cloned.1.call-update
  92.7 0.0 reduce-scatter.2.cloned.1.call-start
  92.7 10.7 %fusion.14 = f32[256,8192]{1,0:T(8,128)} fusion(bf16[768,8192]{1,0:T(8,128)(2,1)} %copy-done, bf16[768,256]{1,0:T(8,128)(2,1)S(1)} %copy-done.3, f32[768]{0:T(1024)S(1)} %add_sqrt_fusion.3), kind=kOutput, calls=%fused_computation.27 | convolution fusion | flops 3221815296 | bytes 21367808 | tf_op jit(solution)/shard_map/dot_general | solution.py:47
  103.4 0.0 reduce-scatter.2.cloned.1.call-update
  103.4 10.7 %psum.31 = f32[8192]{0:T(1024)S(1)} all-reduce(f32[8192]{0:T(1024)S(1)} %get-tuple-element.4), channel_id=1, replica_groups=mesh['dp'=4,'mp'=8] {'dp'}, use_global_device_ids=true, to_apply=%region_12.0 | all-reduce | flops 8192 | bytes 65536 | tf_op jit(solution)/shard_map/psum | solution.py:57
  114.1 51.1 %all-reduce.3.cloned.1.call-done = f32[768,256]{1,0:T(8,128)} async-done(((f32[768,256]{1,0:T(8,128)}), f32[768,256]{1,0:T(8,128)}) %all-reduce.3.cloned.1.call-update) | async-done | bytes 786448 | tf_op jit(solution)/shard_map/psum | solution.py:42
  165.2 1.4 multiply_reduce_fusion.1
  166.7 2.3 %subtract_divide_fusion.1 = f32[768,256]{1,0:T(8,128)} fusion(f32[768,256]{1,0:T(8,128)} %all-reduce.3.cloned.1.call-done, f32[768]{0:T(1024)S(1)} %multiply_reduce_fusion.1, f32[768]{0:T(1024)S(1)} %add_sqrt_fusion.3, bf16[768,256]{1,0:T(8,128)(2,1)S(1)} %copy-done.3), kind=kLoop, calls=%fused_computation.24 | loop fusion | flops 983040 | bytes 1972224 | tf_op jit(solution)/shard_map/div | solution.py:43
  169.0 3.2 %reduce-scatter.2.cloned.1.call-done = f32[64,8192]{1,0:T(8,128)} async-done(((f32[256,8192]{1,0:T(8,128)}), f32[64,8192]{1,0:T(8,128)}) %reduce-scatter.2.cloned.1.call-update) | async-done | bytes 2097168 | tf_op jit(solution)/shard_map/reduce_scatter | solution.py:46
  172.1 3.5 %subtract_divide_fusion = f32[64,8192]{1,0:T(8,128)} fusion(f32[64,8192]{1,0:T(8,128)} %reduce-scatter.2.cloned.1.call-done, f32[8192]{0:T(1024)S(1)} %add_sqrt_fusion.1, f32[8192]{0:T(1024)S(1)} %psum.31, bf16[256,8192]{1,0:T(8,128)(2,1)} %copy-done.1, s32[]{:T(128)S(6)} %select_n.3), kind=kLoop, calls=%fused_computation.16 | loop fusion | flops 2097152 | bytes 5308420 | tf_op jit(solution)/shard_map/div | solution.py:58
  (4 shorter events, 0.0 us)
Async XLA Ops:
  8.0 6.5 %copy-start.3 = (bf16[768,256]{1,0:T(8,128)(2,1)S(1)}, bf16[768,256]{1,0:T(8,128)(2,1)}, u32[]{:S(2)}) copy-start(bf16[768,256]{1,0:T(8,128)(2,1)} %param.6) | copy-start | bytes 1179652
  8.0 7.6 %copy-start.5 = (bf16[768,256]{1,0:T(8,128)(2,1)S(1)}, bf16[768,256]{1,0:T(8,128)(2,1)}, u32[]{:S(2)}) copy-start(bf16[768,256]{1,0:T(8,128)(2,1)} %param.7) | copy-start | bytes 1179652
  8.0 157.2 %all-reduce.3.cloned.1.call-start = ((), (), s32[]{:S(2)}) async-start(), calls=%async_computation.1 | async-start | bytes 1572864 | tf_op jit(solution)/shard_map/psum | solution.py:42
  8.1 6.6 %copy-start.4 = (bf16[256,8192]{1,0:T(8,128)(2,1)S(1)}, bf16[256,8192]{1,0:T(8,128)(2,1)}, u32[]{:S(2)}) copy-start(bf16[256,8192]{1,0:T(8,128)(2,1)} %param.9) | copy-start | bytes 12582916
  14.5 2.0 %copy-start.1 = (bf16[256,8192]{1,0:T(8,128)(2,1)}, bf16[256,8192]{1,0:T(8,128)(2,1)S(1)}, u32[]{:S(2)}) copy-start(bf16[256,8192]{1,0:T(8,128)(2,1)S(1)} %fusion.3) | copy-start | bytes 12582916
  16.5 11.1 %copy-start.6 = (f32[8192]{0:T(1024)S(1)}, f32[8192]{0:T(1024)}, u32[]{:S(2)}) copy-start(f32[8192]{0:T(1024)} %param.10) | copy-start | bytes 98308
  27.7 34.9 %copy-start.7 = (f32[768]{0:T(1024)S(1)}, f32[768]{0:T(1024)}, u32[]{:S(2)}) copy-start(f32[768]{0:T(1024)} %param.11) | copy-start | bytes 9220
  62.6 25.7 %copy-start.2 = (bf16[256,8192]{1,0:T(8,128)(2,1)S(1)}, bf16[256,8192]{1,0:T(8,128)(2,1)}, u32[]{:S(2)}) copy-start(bf16[256,8192]{1,0:T(8,128)(2,1)} %copy-done.1) | copy-start | bytes 12582916
  83.7 4.6 %copy-start = (bf16[768,8192]{1,0:T(8,128)(2,1)}, bf16[768,8192]{1,0:T(8,128)(2,1)S(1)}, u32[]{:S(2)}) copy-start(bf16[768,8192]{1,0:T(8,128)(2,1)S(1)} %get-tuple-element.5) | copy-start | bytes 37748740
  92.7 79.5 %reduce-scatter.2.cloned.1.call-start = ((), (), s32[]{:S(2)}) async-start(), calls=%async_computation.2 | async-start | bytes 10485760 | tf_op jit(solution)/shard_map/reduce_scatter | solution.py:46
Sparse Core Ops, SparseCore 0:
  92.8 72.3 all-reduce.2
Sparse Core Ops, SparseCore 1:
  103.5 68.5 reduce-scatter.1
where the time goes:
time: 183 us
  waiting for transfers between devices  54.3 us (30%)
  matrix products  37.5 us (20%)
  other arithmetic  36 us (20%)
  blocking collectives  34.2 us (19%)
  between operations  15.7 us (9%)
  local copies, waits for them, and re-layouts  5.3 us (3%)
    psum x1, waiting for transfers between devices, local(): grad_unit = lax.psum(partial_value, 'mp')  51.1 us
    psum x1, blocking collectives, local(): lax.psum((jnp.sum(e_student, axis=1), jnp.sum(e_teacher, axis=1)), 'mp')  23.5 us
    reduce_sum x1, other arithmetic, local(): jnp.sum(s_logit * grad_logit.astype(jnp.float32), axis=0)  21.1 us
    dot_general x1, matrix products, local(): t_logit = jnp.dot(z_teacher, w_teacher, preferred_element_type=jnp.float32)  11.4 us
    dot_general x1, matrix products, local(): s_logit = jnp.dot(z_student, w_student, preferred_element_type=jnp.float32)  11.1 us
    dot_general x1, matrix products, local(): lax.dot_general(z_student, grad_logit, (((0,), (0,)), ((), ())), preferre...  10.7 us
    psum x1, blocking collectives, local(): lax.psum(jnp.sum(s_logit * grad_logit.astype(jnp.float32), axis=0), 'dp')  10.7 us
    unnamed x16, local copies, waits for them, and re-layouts  5.3 us
  transfers between devices with their start and end apart: 2, of which 2 were waited for; matrix products, arithmetic and copies ran while one was open for 8% of the time, Pallas kernels for 0%

commit v1 on v0

v1 whole, which is shorter than its diff:
```python
import functools
import math

import jax
import jax.numpy as jnp
from jax import lax
from jax.experimental import pallas as pl
from jax.experimental.pallas import tpu as pltpu
from jax.sharding import PartitionSpec as P

student_temp = 0.1
teacher_temp = 0.04
norm_eps = 1e-06
MESH = pl.DeviceIdType.MESH
LOG2E = math.log2(math.e)
LANES = 128
LAG = 3


def kernel(n_dp, n_mp, tile,
           rs_ref, rt_ref, ps_hbm, pt_hbm, ctr_ref, wt_ref,
           rows_out, protos_hbm,
           ps, pt, e_s, e_t, zs, zt, zst, inv_col, inv_row, z_unit, acc_s, acc_t, sums, sums_in,
           gu, gu_in, gu_all, part, core_in, chip_in,
           load_sem, sum_sem, core_sem, chip_sem, store_sem, rs_sem, ag_sem):
    rows, feats = rs_ref.shape
    steps = ps.shape[0]
    groups = n_dp // 2
    block = feats // n_dp
    piece = rows // n_mp
    dp, mp = lax.axis_index("dp"), lax.axis_index("mp")
    group, core = dp // 2, dp % 2
    other = 1 - core

    def load(i, which):
        cols = pl.ds(pl.multiple_of(i * tile, tile), tile)
        src, dst = ((ps_hbm, ps), (pt_hbm, pt))[which]
        return pltpu.make_async_copy(src.at[:, cols], dst.at[i], load_sem.at[which, i])

    def load_start(i, _):
        load(i, 0).start()
        load(i, 1).start()
        return 0

    lax.fori_loop(0, steps, load_start, 0)

    barrier = pltpu.get_barrier_semaphore()
    pl.semaphore_signal(barrier, inc=1, device_id={"dp": group * 2 + other}, device_id_type=MESH)
    for d in range(1, groups):
        pl.semaphore_signal(
            barrier, inc=1, device_id={"dp": lax.rem(group + d, groups) * 2 + core}, device_id_type=MESH)
    for d in range(1, n_mp):
        pl.semaphore_signal(barrier, inc=1, device_id={"mp": lax.rem(mp + d, n_mp)}, device_id_type=MESH)

    x = rs_ref[...].astype(jnp.float32)
    r_inv = 1.0 / jnp.sqrt(jnp.sum(x * x, axis=1, keepdims=True) + norm_eps)
    zu = x * r_inv
    z_unit[...] = zu
    inv_row[...] = jnp.broadcast_to(r_inv, (rows, LANES))
    zs[...] = zu.astype(jnp.bfloat16)
    zst[...] = zu.T.astype(jnp.bfloat16)
    x = rt_ref[...].astype(jnp.float32)
    zt[...] = (x / jnp.sqrt(jnp.sum(x * x, axis=1, keepdims=True) + norm_eps)).astype(jnp.bfloat16)
    acc_s[...] = jnp.zeros_like(acc_s)
    acc_t[...] = jnp.zeros_like(acc_t)

    def lanes(e):
        return sum(e[:, k * LANES:(k + 1) * LANES] for k in range(tile // LANES))

    def forward(i, _):
        load(i, 0).wait()
        load(i, 1).wait()
        v = ps[i].astype(jnp.float32)
        c_inv = 1.0 / jnp.sqrt(jnp.sum(v * v, axis=0, keepdims=True) + norm_eps)
        inv_col[i] = c_inv
        w = (v * c_inv).astype(jnp.bfloat16)
        ps[i] = w
        s = jnp.dot(zs[...], w, preferred_element_type=jnp.float32)
        es = jnp.exp2((s - 1.0) * (LOG2E / student_temp))
        acc_s[...] += lanes(es)
        e_s[i] = es.astype(jnp.bfloat16)
        u = pt[i].astype(jnp.float32)
        u_inv = 1.0 / jnp.sqrt(jnp.sum(u * u, axis=0, keepdims=True) + norm_eps)
        wt = (u * u_inv).astype(jnp.bfloat16)
        t = jnp.dot(zt[...], wt, preferred_element_type=jnp.float32)
        shift = ctr_ref[:, pl.ds(pl.multiple_of(i * tile, tile), tile)] + 1.0
        et = jnp.exp2((t - shift) * (LOG2E / teacher_temp))
        acc_t[...] += lanes(et)
        e_t[i] = et.astype(jnp.bfloat16)
        return 0

    lax.fori_loop(0, steps, forward, 0)

    sums[0:1, :] = jnp.sum(acc_s[...].T, axis=0, keepdims=True)
    sums[1:2, :] = jnp.sum(acc_t[...].T, axis=0, keepdims=True)
    pl.semaphore_wait(barrier, 1 + (groups - 1) + (n_mp - 1))

    def sum_copy(d):
        return pltpu.make_async_remote_copy(
            src_ref=sums, dst_ref=sums_in.at[d], send_sem=sum_sem.at[0, d], recv_sem=sum_sem.at[1, d],
            device_id={"mp": lax.rem(mp + d, n_mp)}, device_id_type=MESH)

    for d in range(1, n_mp):
        sum_copy(d).start()
    total = sums[...]
    for d in range(1, n_mp):
        sum_copy(d).wait()
        total = total + sums_in[d]
    scale = wt_ref[...] / student_temp / total
    acc_s[...] = jnp.broadcast_to(scale[0:1, :], (LANES, rows)).T
    acc_t[...] = jnp.broadcast_to(scale[1:2, :], (LANES, rows)).T
    gu[...] = jnp.zeros_like(gu)

    def rows_of(q, c):
        return pl.ds(pl.multiple_of((q * 2 + c) * block, block), block)

    def core_copy(i, q):
        return pltpu.make_async_remote_copy(
            src_ref=part.at[i, rows_of(q, other)], dst_ref=core_in.at[i, q],
            send_sem=core_sem.at[0, i, q], recv_sem=core_sem.at[1, i, q],
            device_id={"dp": group * 2 + other}, device_id_type=MESH)

    def chip_copy(i, d):
        to = lax.rem(group + d, groups)
        return pltpu.make_async_remote_copy(
            src_ref=part.at[i, rows_of(to, core)], dst_ref=chip_in.at[i, d - 1],
            send_sem=chip_sem.at[0, i, d - 1], recv_sem=chip_sem.at[1, i, d - 1],
            device_id={"dp": to * 2 + core}, device_id_type=MESH)

    def forward_chip(i):
        for q in range(groups):
            core_copy(i, q).wait()
        for d in range(groups):
            q = lax.rem(group + d, groups)
            part[i, rows_of(q, core)] += core_in[i, q]
            if d:
                chip_copy(i, d).start()

    def wide(a):
        return jnp.concatenate([a] * (tile // LANES), axis=1)

    def backward(i, _):
        a = wide(acc_s[...]) * e_s[i].astype(jnp.float32)
        b = wide(acc_t[...]) * e_t[i].astype(jnp.float32)
        g = (a - b).astype(jnp.bfloat16)
        w = ps[i]
        gw = jnp.dot(zst[...], g, preferred_element_type=jnp.float32)
        wf = w.astype(jnp.float32)
        part[i] = (gw - wf * jnp.sum(wf * gw, axis=0, keepdims=True)) * inv_col[i]
        for q in range(groups):
            core_copy(i, q).start()
        gu[...] += lax.dot_general(g, w, (((1,), (1,)), ((), ())), preferred_element_type=jnp.float32)

        @pl.when(i >= LAG)
        def _():
            forward_chip(i - LAG)
        return 0

    lax.fori_loop(0, steps, backward, 0)

    g_all = gu[...]
    zu = z_unit[...]
    dots = jnp.sum(zu * g_all, axis=1, keepdims=True)
    gu[...] = (g_all - zu * dots) * inv_row[:, 0:1]

    def piece_of(j):
        return pl.ds(pl.multiple_of(j * piece, piece), piece)

    def rs_copy(d):
        to = lax.rem(mp + d, n_mp)
        return pltpu.make_async_remote_copy(
            src_ref=gu.at[piece_of(to)], dst_ref=gu_in.at[d], send_sem=rs_sem.at[0, d], recv_sem=rs_sem.at[1, d],
            device_id={"mp": to}, device_id_type=MESH)

    def ag_copy(d):
        return pltpu.make_async_remote_copy(
            src_ref=gu_in.at[0], dst_ref=gu_all.at[d], send_sem=ag_sem.at[0, d], recv_sem=ag_sem.at[1, d],
            device_id={"mp": lax.rem(mp + d, n_mp)}, device_id_type=MESH)

    for d in range(1, n_mp):
        rs_copy(d).start()

    def tail(i, _):
        forward_chip(i)
        return 0

    lax.fori_loop(max(steps - LAG, 0), steps, tail, 0)

    def store(i):
        cols = pl.ds(pl.multiple_of(i * tile, tile), tile)
        return pltpu.make_async_copy(part.at[i, rows_of(group, core)], protos_hbm.at[:, cols], store_sem.at[i])

    def drain(i, _):
        own = part[i, rows_of(group, core)]
        for d in range(1, groups):
            chip_copy(i, d).wait()
            own = own + chip_in[i, d - 1]
        part[i, rows_of(group, core)] = own
        store(i).start()
        return 0

    early = steps * 5 // 8
    lax.fori_loop(0, early, drain, 0)

    mine = gu[piece_of(mp)]
    for d in range(1, n_mp):
        rs_copy(d).wait()
        mine = mine + gu_in[d]
    gu_in[0] = mine
    for d in range(1, n_mp):
        ag_copy(d).start()
    rows_out[piece_of(mp)] = mine

    lax.fori_loop(early, steps, drain, 0)

    for d in range(1, n_mp):
        ag_copy(d).wait()
        rows_out[piece_of(lax.rem(mp - d + n_mp, n_mp))] = gu_all[d]

    def stored(i, _):
        store(i).wait()
        return 0

    lax.fori_loop(0, steps, stored, 0)


def solution(mesh):
    n_dp, n_mp = mesh.shape["dp"], mesh.shape["mp"]
    groups = n_dp // 2

    def local(student_rows, teacher_rows, student_protos, teacher_protos, center, row_weight):
        rows, feats = student_rows.shape
        cols = student_protos.shape[1]
        tile = math.gcd(cols, 256)
        steps = cols // tile
        block, piece = feats // n_dp, rows // n_mp
        f32, bf16 = jnp.float32, jnp.bfloat16
        vmem, anywhere = pl.BlockSpec(memory_space=pltpu.VMEM), pl.BlockSpec(memory_space=pl.ANY)
        dma = pltpu.SemaphoreType.DMA
        return pl.pallas_call(
            functools.partial(kernel, n_dp, n_mp, tile),
            name="head_backward",
            out_shape=(jax.ShapeDtypeStruct((rows, feats), f32), jax.ShapeDtypeStruct((block, cols), f32)),
            in_specs=[vmem, vmem, anywhere, anywhere, vmem, vmem],
            out_specs=(vmem, anywhere),
            scratch_shapes=[
                pltpu.VMEM((steps, feats, tile), bf16),
                pltpu.VMEM((steps, feats, tile), bf16),
                pltpu.VMEM((steps, rows, tile), bf16),
                pltpu.VMEM((steps, rows, tile), bf16),
                pltpu.VMEM((rows, feats), bf16),
                pltpu.VMEM((rows, feats), bf16),
                pltpu.VMEM((feats, rows), bf16),
                pltpu.VMEM((steps, 1, tile), f32),
                pltpu.VMEM((rows, LANES), f32),
                pltpu.VMEM((rows, feats), f32),
                pltpu.VMEM((rows, LANES), f32),
                pltpu.VMEM((rows, LANES), f32),
                pltpu.VMEM((2, rows), f32),
                pltpu.VMEM((n_mp, 2, rows), f32),
                pltpu.VMEM((rows, feats), f32),
                pltpu.VMEM((n_mp, piece, feats), f32),
                pltpu.VMEM((n_mp, piece, feats), f32),
                pltpu.VMEM((steps, feats, tile), f32),
                pltpu.VMEM((steps, groups, block, tile), f32),
                pltpu.VMEM((steps, groups - 1, block, tile), f32),
                dma((2, steps)),
                dma((2, n_mp)),
                dma((2, steps, groups)),
                dma((2, steps, groups - 1)),
                dma((steps,)),
                dma((2, n_mp)),
                dma((2, n_mp)),
            ],
            compiler_params=pltpu.CompilerParams(
                collective_id=0, has_side_effects=True, vmem_limit_bytes=67043328),
        )(student_rows, teacher_rows, student_protos, teacher_protos, center[None, :], row_weight[None, :])

    placed = (P("dp", None), P("dp", None), P(None, "mp"), P(None, "mp"), P("mp"), P("dp"))
    return jax.shard_map(
        local, mesh=mesh, in_specs=placed, out_specs=(P("dp", None), P("dp", "mp")), check_vma=False
    )
```

time: 183 us -> 89.1 us (0.49)
  the two profiles are of different devices: /device:TPU:0 before, /device:TPU:31 now
where the time goes in v1:
time: 89.1 us; the launch traced here: 88.9 us
  Pallas kernels  81.8 us (92%)
  local copies, waits for them, and re-layouts  6.39 us (7%)
    pallas_call x1, Pallas kernels, local(): pl.pallas_call(functools.partial(kernel, n_dp, n_mp, tile), name='head_ba...  81.8 us
    unnamed x2, local copies, waits for them, and re-layouts  5.12 us

profile of v1, /device:TPU:31, one launch (start us, length us, event | category | flops | bytes accessed | tf_op | source)
XLA Modules:
  0.0 88.9 jit_solution(11701762374949846284)
XLA Ops:
  0.6 1.3 %broadcast_in_dim.7.wt_ref = f32[1,768]{1,0:T(1,128)} reshape(f32[768]{0:T(1024)} %param.11) | data formatting | bytes 6144 | tf_op jit(solution)/shard_map/broadcast_in_dim | solution.py:277
  1.9 81.8 %head_backward.1 = (f32[768,256]{1,0:T(8,128)}, f32[64,8192]{1,0:T(8,128)}) custom-call(bf16[768,256]{1,0:T(8,128)(2,1)} %rs_ref.1, bf16[768,256]{1,0:T(8,128)(2,1)} %rt_ref.1, bf16[256,8192]{1,0:T(8,128)(2,1)} %ps_hbm.1, bf16[256,8192]{1,0:T(8,128)(2,1)} %pt_hbm.1, f32[1,8192]{1,0:T(1,128)} %bitcast.1, f32[1,768]{1,0:T(1,128)} %broadcast_in_dim.7.wt_ref), custom_call_target="tpu_custom_call" | custom-call | tf_op jit(solution)/shard_map/head_backward/pallas_call | solution.py:240
  83.7 2.1 %copy.10 = f32[768,256]{1,0:T(8,128)} copy(f32[768,256]{1,0:T(8,128)} %get-tuple-element.4) | data formatting | bytes 1572864
  85.8 3.1 %copy.11 = f32[64,8192]{1,0:T(8,128)} copy(f32[64,8192]{1,0:T(8,128)} %get-tuple-element.5) | data formatting | bytes 4194304

commit v2 on v1

--- a/solution.py
+++ b/solution.py
@@ -14,7 +14,7 @@
 MESH = pl.DeviceIdType.MESH
 LOG2E = math.log2(math.e)
 LANES = 128
-LAG = 3
+LAG = 2
 
 
 def kernel(n_dp, n_mp, tile,
@@ -76,15 +76,15 @@
         w = (v * c_inv).astype(jnp.bfloat16)
         ps[i] = w
         s = jnp.dot(zs[...], w, preferred_element_type=jnp.float32)
-        es = jnp.exp2((s - 1.0) * (LOG2E / student_temp))
+        es = jnp.exp2(s * (LOG2E / student_temp))
         acc_s[...] += lanes(es)
         e_s[i] = es.astype(jnp.bfloat16)
         u = pt[i].astype(jnp.float32)
         u_inv = 1.0 / jnp.sqrt(jnp.sum(u * u, axis=0, keepdims=True) + norm_eps)
         wt = (u * u_inv).astype(jnp.bfloat16)
         t = jnp.dot(zt[...], wt, preferred_element_type=jnp.float32)
-        shift = ctr_ref[:, pl.ds(pl.multiple_of(i * tile, tile), tile)] + 1.0
-        et = jnp.exp2((t - shift) * (LOG2E / teacher_temp))
+        shift = ctr_ref[:, pl.ds(pl.multiple_of(i * tile, tile), tile)] * (LOG2E / teacher_temp)
+        et = jnp.exp2(t * (LOG2E / teacher_temp) - shift)
         acc_t[...] += lanes(et)
         e_t[i] = et.astype(jnp.bfloat16)
         return 0
@@ -231,7 +231,7 @@
     def local(student_rows, teacher_rows, student_protos, teacher_protos, center, row_weight):
         rows, feats = student_rows.shape
         cols = student_protos.shape[1]
-        tile = math.gcd(cols, 256)
+        tile = math.gcd(cols, 512)
         steps = cols // tile
         block, piece = feats // n_dp, rows // n_mp
         f32, bf16 = jnp.float32, jnp.bfloat16

time: 89.1 us -> 82 us (0.920)
  the two profiles are of different devices: /device:TPU:31 before, /device:TPU:0 now
where the time goes in v2:
time: 82 us; the launch traced here: 81.8 us
  Pallas kernels  74.7 us (91%)
  local copies, waits for them, and re-layouts  6.39 us (8%)
    pallas_call x1, Pallas kernels, local(): pl.pallas_call(functools.partial(kernel, n_dp, n_mp, tile), name='head_ba...  74.7 us
    unnamed x2, local copies, waits for them, and re-layouts  5.12 us

profile of v2, /device:TPU:0, one launch (start us, length us, event | category | flops | bytes accessed | tf_op | source)
XLA Modules:
  0.0 81.8 jit_solution(14420783540352927094)
XLA Ops:
  0.6 1.3 %broadcast_in_dim.7.wt_ref = f32[1,768]{1,0:T(1,128)} reshape(f32[768]{0:T(1024)} %param.11) | data formatting | bytes 6144 | tf_op jit(solution)/shard_map/broadcast_in_dim | solution.py:277
  1.9 74.7 %head_backward.1 = (f32[768,256]{1,0:T(8,128)}, f32[64,8192]{1,0:T(8,128)}) custom-call(bf16[768,256]{1,0:T(8,128)(2,1)} %rs_ref.1, bf16[768,256]{1,0:T(8,128)(2,1)} %rt_ref.1, bf16[256,8192]{1,0:T(8,128)(2,1)} %ps_hbm.1, bf16[256,8192]{1,0:T(8,128)(2,1)} %pt_hbm.1, f32[1,8192]{1,0:T(1,128)} %bitcast.1, f32[1,768]{1,0:T(1,128)} %broadcast_in_dim.7.wt_ref), custom_call_target="tpu_custom_call" | custom-call | tf_op jit(solution)/shard_map/head_backward/pallas_call | solution.py:240
  76.6 2.1 %copy.10 = f32[768,256]{1,0:T(8,128)} copy(f32[768,256]{1,0:T(8,128)} %get-tuple-element.4) | data formatting | bytes 1572864
  78.7 3.1 %copy.11 = f32[64,8192]{1,0:T(8,128)} copy(f32[64,8192]{1,0:T(8,128)} %get-tuple-element.5) | data formatting | bytes 4194304
